TPU v7x, 32 devices: a whole 2x2x4 slice. The times are simulated.
32 devices in a mesh: fsdp: 2 (over core), ctx: 4 (over y, x), tp: 4 (over z).
Axes of the slice: x: 2, y: 2, z: 4, core: 2. Of those that a mesh axis runs over, the one named last changes fastest.
Arguments:
- x_prompt: bfloat16 [2, 1024, 1024], P('fsdp', 'ctx'), may hold values from -6 to 6
- x_cont: bfloat16 [2, 12, 256, 1024], P('fsdp', 'ctx'), may hold values from -6 to 6
- cont_start: int32 [2, 12], P('fsdp', 'ctx'), may hold values from 512 to 1024
- w_qkv: bfloat16 [1024, 3, 1024], P(('fsdp', 'ctx'), None, 'tp'), may hold values from -0.1875 to 0.1875
- qkv_bias: bfloat16 [3, 1024], P(None, 'tp'), may hold values from -3 to 3
- w_dense: bfloat16 [1024, 1024], P('tp', ('fsdp', 'ctx')), may hold values from -0.75 to 0.75
- dense_bias: bfloat16 [1024], P(('fsdp', 'ctx')), may hold values from -3 to 3
- w_fc1: bfloat16 [1024, 4096], P(('fsdp', 'ctx'), 'tp'), may hold values from -0.1875 to 0.1875
- fc1_bias: bfloat16 [4096], P('tp'), may hold values from -3 to 3
- w_fc2: bfloat16 [4096, 1024], P('tp', ('fsdp', 'ctx')), may hold values from -0.09375 to 0.09375
- fc2_bias: bfloat16 [1024], P(('fsdp', 'ctx')), may hold values from -3 to 3
- ln1_gain: bfloat16 [1024], P(('fsdp', 'ctx')), may hold values from 0.099609375 to 1.8984375
- ln1_bias: bfloat16 [1024], P(('fsdp', 'ctx')), may hold values from -2 to 2
- ln2_gain: bfloat16 [1024], P(('fsdp', 'ctx')), may hold values from 0.099609375 to 1.8984375
- ln2_bias: bfloat16 [1024], P(('fsdp', 'ctx')), may hold values from -2 to 2
- dy_prompt: bfloat16 [2, 1024, 1024], P('fsdp', 'ctx'), may hold values from -6 to 6
- dy_cont: bfloat16 [2, 12, 256, 1024], P('fsdp', 'ctx'), may hold values from -6 to 6
Outputs:
- y_prompt: float32 [2, 1024, 1024], P('fsdp', 'ctx')
- y_cont: float32 [2, 12, 256, 1024], P('fsdp', 'ctx')
- dx_prompt: float32 [2, 1024, 1024], P('fsdp', 'ctx')
- dx_cont: float32 [2, 12, 256, 1024], P('fsdp', 'ctx')
- d_w_qkv: float32 [1024, 3, 1024], P(('fsdp', 'ctx'), None, 'tp')
- d_qkv_bias: float32 [3, 1024], P(None, 'tp')
- d_w_dense: float32 [1024, 1024], P('tp', ('fsdp', 'ctx'))
- d_dense_bias: float32 [1024], P(('fsdp', 'ctx'))
- d_w_fc1: float32 [1024, 4096], P(('fsdp', 'ctx'), 'tp')
- d_fc1_bias: float32 [4096], P('tp')
- d_w_fc2: float32 [4096, 1024], P('tp', ('fsdp', 'ctx'))
- d_fc2_bias: float32 [1024], P(('fsdp', 'ctx'))
- d_ln1_gain: float32 [1024], P(('fsdp', 'ctx'))
- d_ln1_bias: float32 [1024], P(('fsdp', 'ctx'))
- d_ln2_gain: float32 [1024], P(('fsdp', 'ctx'))
- d_ln2_bias: float32 [1024], P(('fsdp', 'ctx'))
Inputs may be any that keep to these rules, and one draw needn't show every extreme that they name: `cont_start`: a continuation follows the prompt tokens before its first position.
All inputs are finite; a program needn't handle non-finite values.
Results may differ from a plain program's by a relative error of at most 0.012.
Values may be sent and summed in bfloat16 or wider, within the bound.
A program may use at most 192 MiB of HBM per device.

v0:
```python
import jax
import jax.numpy as jnp
from jax import lax
from jax.sharding import PartitionSpec as P

HD = 64
ROT = 16
EPS = 1e-05


def layer_norm(inputs, norm_gain, norm_shift):
    row_mean = jnp.mean(inputs, axis=-1, keepdims=True)
    centered = inputs - row_mean
    variance = jnp.mean(centered * centered, axis=-1, keepdims=True)
    return centered * lax.rsqrt(variance + EPS) * norm_gain + norm_shift


def norm_pair(inputs, gain_one, shift_one, gain_two, shift_two):
    return (layer_norm(inputs, gain_one, shift_one), layer_norm(inputs, gain_two, shift_two))


def exact_gelu(values):
    return jax.nn.gelu(values, approximate=False)


def rotary_tables(positions):
    freq_index = jnp.arange(ROT // 2).astype(jnp.float32)
    inverse = jnp.power(10000.0, -2.0 * freq_index / ROT)
    phase = positions.astype(jnp.float32)[..., None] * inverse
    cos_half = jnp.cos(phase)
    sin_half = jnp.sin(phase)
    return (
        jnp.concatenate([cos_half, cos_half], axis=-1),
        jnp.concatenate([sin_half, sin_half], axis=-1),
    )


def rotate(inputs, cos_t, sin_t):
    leading = inputs[..., :ROT]
    half_rot = ROT // 2
    turned = jnp.concatenate([-leading[..., half_rot:], leading[..., :half_rot]], axis=-1)
    return jnp.concatenate([leading * cos_t + turned * sin_t, inputs[..., ROT:]], axis=-1)


def masked_scores(
    queries, all_keys, key_limit, query_slot, query_offs, prompt_len, key_slot, key_offs
):
    raw_scores = jnp.einsum("qhd,khd->hqk", queries, all_keys, preferred_element_type=jnp.float32)
    key_index = jnp.arange(all_keys.shape[0], dtype=jnp.int32)
    near_keys = key_index[None, :] < key_limit[:, None]
    own_keys = (key_slot[None, :] == query_slot[:, None]) & (
        key_offs[None, :] <= query_offs[:, None]
    )
    allowed = jnp.where((key_index < prompt_len)[None, :], near_keys, own_keys)
    return jnp.where(allowed[None], raw_scores * 0.125, -1e30)


def on_device(
    x_prompt,
    x_cont,
    cont_start,
    w_qkv,
    qkv_bias,
    w_dense,
    dense_bias,
    w_fc1,
    fc1_bias,
    w_fc2,
    fc2_bias,
    ln1_gain,
    ln1_bias,
    ln2_gain,
    ln2_bias,
    dy_prompt,
    dy_cont,
):
    gathered = (
        lax.all_gather(w_qkv, ("fsdp", "ctx"), axis=0, tiled=True),
        lax.all_gather(w_dense, ("fsdp", "ctx"), axis=1, tiled=True),
        lax.all_gather(w_fc1, ("fsdp", "ctx"), axis=0, tiled=True),
        lax.all_gather(w_fc2, ("fsdp", "ctx"), axis=1, tiled=True),
        lax.all_gather(dense_bias, ("fsdp", "ctx"), axis=0, tiled=True),
        lax.all_gather(fc2_bias, ("fsdp", "ctx"), axis=0, tiled=True),
        lax.all_gather(ln1_gain, ("fsdp", "ctx"), axis=0, tiled=True),
        lax.all_gather(ln1_bias, ("fsdp", "ctx"), axis=0, tiled=True),
        lax.all_gather(ln2_gain, ("fsdp", "ctx"), axis=0, tiled=True),
        lax.all_gather(ln2_bias, ("fsdp", "ctx"), axis=0, tiled=True),
    )
    qkv_full, dense_full, up_full, down_full = (gathered[0], gathered[1], gathered[2], gathered[3])
    dense_shift = gathered[4].astype(jnp.float32)
    down_shift = gathered[5].astype(jnp.float32)
    gain_one = gathered[6].astype(jnp.float32)
    shift_one = gathered[7].astype(jnp.float32)
    gain_two = gathered[8].astype(jnp.float32)
    shift_two = gathered[9].astype(jnp.float32)
    p_rows = x_prompt.shape[1]
    cont_count = x_cont.shape[1]
    cont_len = x_cont.shape[2]
    model_width = x_prompt.shape[2]
    row_count = p_rows + cont_count * cont_len
    prompt_len = p_rows * lax.axis_size("ctx")
    local_cols = qkv_full.shape[2]
    head_count = local_cols // HD
    piece_index = lax.axis_index("ctx")
    inputs = jnp.concatenate(
        [x_prompt[0], x_cont[0].reshape(cont_count * cont_len, model_width)], axis=0
    ).astype(jnp.float32)
    offsets = jnp.arange(cont_len, dtype=jnp.int32)
    prompt_pos = piece_index * p_rows + jnp.arange(p_rows, dtype=jnp.int32)
    starts = cont_start[0]
    cont_pos = (starts[:, None] + offsets[None, :]).reshape(cont_count * cont_len)
    positions = jnp.concatenate([prompt_pos, cont_pos])
    key_limit = jnp.concatenate([prompt_pos + 1, jnp.repeat(starts, cont_len)])
    own_slot = jnp.repeat(jnp.arange(cont_count, dtype=jnp.int32), cont_len)
    own_offs = jnp.tile(offsets, cont_count)
    query_slot = jnp.concatenate([jnp.full((p_rows,), -1, jnp.int32), own_slot])
    query_offs = jnp.concatenate([jnp.zeros((p_rows,), jnp.int32), own_offs])
    key_slot = jnp.concatenate([jnp.full((prompt_len,), -1, jnp.int32), own_slot])
    key_offs = jnp.concatenate([jnp.zeros((prompt_len,), jnp.int32), own_offs])
    cos_t, sin_t = rotary_tables(positions)
    cos_t = cos_t[:, None, :]
    sin_t = sin_t[:, None, :]
    norm_one, norm_two = norm_pair(inputs, gain_one, shift_one, gain_two, shift_two)
    ln_one = norm_one.astype(jnp.bfloat16)
    ln_two = norm_two.astype(jnp.bfloat16)
    qkv_flat = qkv_full.reshape(model_width, 3 * local_cols)
    projected = jnp.dot(ln_one, qkv_flat, preferred_element_type=jnp.float32) + qkv_bias.reshape(
        3 * local_cols
    ).astype(jnp.float32)
    projected = projected.reshape(row_count, 3, head_count, HD)
    queries = rotate(projected[:, 0], cos_t, sin_t).astype(jnp.bfloat16)
    keys_own = rotate(projected[:, 1], cos_t, sin_t).astype(jnp.bfloat16)
    values_own = projected[:, 2].astype(jnp.bfloat16)
    prompt_keys, prompt_values = (
        lax.all_gather(keys_own[:p_rows].reshape(p_rows, local_cols), "ctx", axis=0, tiled=True),
        lax.all_gather(values_own[:p_rows].reshape(p_rows, local_cols), "ctx", axis=0, tiled=True),
    )
    all_keys = jnp.concatenate(
        [prompt_keys.reshape(prompt_len, head_count, HD), keys_own[p_rows:]], axis=0
    )
    all_values = jnp.concatenate(
        [prompt_values.reshape(prompt_len, head_count, HD), values_own[p_rows:]], axis=0
    )
    scores = masked_scores(
        queries, all_keys, key_limit, query_slot, query_offs, prompt_len, key_slot, key_offs
    )
    highest = jnp.max(scores, axis=-1, keepdims=True)
    log_total = highest + jnp.log(jnp.sum(jnp.exp(scores - highest), axis=-1, keepdims=True))
    probs_low = jnp.exp(scores - log_total).astype(jnp.bfloat16)
    attended = jnp.einsum("hqk,khd->qhd", probs_low, all_values, preferred_element_type=jnp.float32)
    attended_low = attended.reshape(row_count, local_cols).astype(jnp.bfloat16)
    attn_part = jnp.dot(attended_low, dense_full, preferred_element_type=jnp.float32)
    hidden = jnp.dot(ln_two, up_full, preferred_element_type=jnp.float32) + fc1_bias.astype(
        jnp.float32
    )
    active_low = exact_gelu(hidden).astype(jnp.bfloat16)
    mlp_part = jnp.dot(active_low, down_full, preferred_element_type=jnp.float32)
    attn_total = lax.psum(attn_part, "tp")
    mlp_total = lax.psum(mlp_part.astype(jnp.bfloat16), "tp").astype(jnp.float32)
    mixed = attn_total + mlp_total
    output = inputs + mixed + dense_shift + down_shift
    again = (
        lax.all_gather(w_qkv, ("fsdp", "ctx"), axis=0, tiled=True),
        lax.all_gather(w_dense, ("fsdp", "ctx"), axis=1, tiled=True),
        lax.all_gather(w_fc1, ("fsdp", "ctx"), axis=0, tiled=True),
        lax.all_gather(w_fc2, ("fsdp", "ctx"), axis=1, tiled=True),
    )
    qkv_flat = again[0].reshape(model_width, 3 * local_cols)
    dense_full, up_full, down_full = (again[1], again[2], again[3])
    grad_out = jnp.concatenate(
        [dy_prompt[0], dy_cont[0].reshape(cont_count * cont_len, model_width)], axis=0
    )
    grad_dense = jnp.dot(attended_low.T, grad_out, preferred_element_type=jnp.float32)
    grad_down = jnp.dot(active_low.T, grad_out, preferred_element_type=jnp.float32)
    grad_shift = jnp.sum(grad_out.astype(jnp.float32), axis=0)
    grad_attended = (
        jnp.dot(grad_out, dense_full.T, preferred_element_type=jnp.float32)
        .astype(jnp.bfloat16)
        .reshape(row_count, head_count, HD)
    )
    scores = masked_scores(
        queries, all_keys, key_limit, query_slot, query_offs, prompt_len, key_slot, key_offs
    )
    probs = jnp.exp(scores - log_total)
    probs_low = probs.astype(jnp.bfloat16)
    grad_probs = jnp.einsum(
        "qhd,khd->hqk", grad_attended, all_values, preferred_element_type=jnp.float32
    )
    inner = jnp.sum(probs * grad_probs, axis=-1, keepdims=True)
    grad_scores = (probs * (grad_probs - inner)).astype(jnp.bfloat16)
    grad_queries = (
        jnp.einsum("hqk,khd->qhd", grad_scores, all_keys, preferred_element_type=jnp.float32)
        * 0.125
    )
    grad_keys = (
        jnp.einsum("hqk,qhd->khd", grad_scores, queries, preferred_element_type=jnp.float32) * 0.125
    )
    grad_values = jnp.einsum(
        "hqk,qhd->khd", probs_low, grad_attended, preferred_element_type=jnp.float32
    )
    prompt_key_grads, prompt_value_grads = (
        lax.psum_scatter(
            grad_keys[:prompt_len].reshape(prompt_len, local_cols),
            "ctx",
            scatter_dimension=0,
            tiled=True,
        ),
        lax.psum_scatter(
            grad_values[:prompt_len].reshape(prompt_len, local_cols),
            "ctx",
            scatter_dimension=0,
            tiled=True,
        ),
    )
    grad_keys = jnp.concatenate(
        [prompt_key_grads.reshape(p_rows, head_count, HD), grad_keys[prompt_len:]], axis=0
    )
    grad_values = jnp.concatenate(
        [prompt_value_grads.reshape(p_rows, head_count, HD), grad_values[prompt_len:]], axis=0
    )
    grad_projected = jnp.stack(
        [rotate(grad_queries, cos_t, -sin_t), rotate(grad_keys, cos_t, -sin_t), grad_values], axis=1
    )
    grad_proj_low = grad_projected.reshape(row_count, 3 * local_cols).astype(jnp.bfloat16)
    grad_qkv = jnp.dot(ln_one.T, grad_proj_low, preferred_element_type=jnp.float32).reshape(
        model_width, 3, local_cols
    )
    grad_qkv_bias = jnp.sum(grad_proj_low.astype(jnp.float32), axis=0).reshape(3, local_cols)
    grad_norm_one = jnp.dot(grad_proj_low, qkv_flat.T, preferred_element_type=jnp.float32)
    grad_active = jnp.dot(grad_out, down_full.T, preferred_element_type=jnp.float32)
    gelu_back = jax.vjp(exact_gelu, hidden)[1]
    grad_hidden_low = gelu_back(grad_active)[0].astype(jnp.bfloat16)
    grad_up = jnp.dot(ln_two.T, grad_hidden_low, preferred_element_type=jnp.float32)
    grad_up_bias = jnp.sum(grad_hidden_low.astype(jnp.float32), axis=0)
    grad_norm_two = jnp.dot(grad_hidden_low, up_full.T, preferred_element_type=jnp.float32)
    norm_back = jax.vjp(norm_pair, inputs, gain_one, shift_one, gain_two, shift_two)[1]
    full_one = lax.psum(grad_norm_one, "tp")
    full_two = lax.psum(grad_norm_two, "tp")
    grad_in, grad_gain_one, grad_shift_one, grad_gain_two, grad_shift_two = norm_back(
        (full_one, full_two)
    )
    grad_inputs = grad_in + grad_out.astype(jnp.float32)
    owned = (
        lax.psum_scatter(grad_qkv, ("fsdp", "ctx"), scatter_dimension=0, tiled=True),
        lax.psum_scatter(grad_dense, ("fsdp", "ctx"), scatter_dimension=1, tiled=True),
        lax.psum_scatter(grad_up, ("fsdp", "ctx"), scatter_dimension=0, tiled=True),
        lax.psum_scatter(grad_down, ("fsdp", "ctx"), scatter_dimension=1, tiled=True),
        lax.psum_scatter(grad_shift, ("fsdp", "ctx"), scatter_dimension=0, tiled=True),
        lax.psum_scatter(grad_gain_one, ("fsdp", "ctx"), scatter_dimension=0, tiled=True),
        lax.psum_scatter(grad_shift_one, ("fsdp", "ctx"), scatter_dimension=0, tiled=True),
        lax.psum_scatter(grad_gain_two, ("fsdp", "ctx"), scatter_dimension=0, tiled=True),
        lax.psum_scatter(grad_shift_two, ("fsdp", "ctx"), scatter_dimension=0, tiled=True),
    )
    bias_qkv_total, bias_up_total = lax.psum((grad_qkv_bias, grad_up_bias), ("fsdp", "ctx"))
    y_prompt = output[:p_rows][None]
    y_cont = output[p_rows:].reshape(1, cont_count, cont_len, model_width)
    dx_prompt = grad_inputs[:p_rows][None]
    dx_cont = grad_inputs[p_rows:].reshape(1, cont_count, cont_len, model_width)
    return (
        y_prompt,
        y_cont,
        dx_prompt,
        dx_cont,
        owned[0],
        bias_qkv_total,
        owned[1],
        owned[4],
        owned[2],
        bias_up_total,
        owned[3],
        owned[4],
        owned[5],
        owned[6],
        owned[7],
        owned[8],
    )


def solution(mesh):
    placed = (
        P("fsdp", "ctx", None),
        P("fsdp", "ctx", None, None),
        P("fsdp", "ctx"),
        P(("fsdp", "ctx"), None, "tp"),
        P(None, "tp"),
        P("tp", ("fsdp", "ctx")),
        P(("fsdp", "ctx")),
        P(("fsdp", "ctx"), "tp"),
        P("tp"),
        P("tp", ("fsdp", "ctx")),
        P(("fsdp", "ctx")),
        P(("fsdp", "ctx")),
        P(("fsdp", "ctx")),
        P(("fsdp", "ctx")),
        P(("fsdp", "ctx")),
        P("fsdp", "ctx", None),
        P("fsdp", "ctx", None, None),
    )
    return jax.shard_map(
        on_device,
        mesh=mesh,
        in_specs=placed,
        out_specs=(
            P("fsdp", "ctx", None),
            P("fsdp", "ctx", None, None),
            P("fsdp", "ctx", None),
            P("fsdp", "ctx", None, None),
            P(("fsdp", "ctx"), None, "tp"),
            P(None, "tp"),
            P("tp", ("fsdp", "ctx")),
            P(("fsdp", "ctx")),
            P(("fsdp", "ctx"), "tp"),
            P("tp"),
            P("tp", ("fsdp", "ctx")),
            P(("fsdp", "ctx")),
            P(("fsdp", "ctx")),
            P(("fsdp", "ctx")),
            P(("fsdp", "ctx")),
            P(("fsdp", "ctx")),
        ),
        check_vma=False,
    )
```

profile of v0, /device:TPU:0, one launch (start us, length us, event | category | flops | bytes accessed | tf_op | source)
XLA Modules:
  0.0 1037.2 jit_solution(66057958732764653)
XLA Ops:
  18.0 14.7 %all-gather = bf16[8,1,128]{2,1,0:T(2,128)(2,1)S(1)} all-gather(bf16[1,1,128]{2,1,0:T(2,128)(2,1)S(1)} %bitcast.150), channel_id=1, replica_groups=mesh['fsdp'=2,'ctx'=4,'tp'=4] {'fsdp','ctx'}, dimensions={0}, use_global_device_ids=true | all-gather | bytes 2304 | tf_op jit(solution)/shard_map/all_gather | solution.py:84
  32.7 13.2 %all-gather.1 = bf16[8,1,128]{2,1,0:T(2,128)(2,1)S(1)} all-gather(bf16[1,1,128]{2,1,0:T(2,128)(2,1)S(1)} %bitcast.151), channel_id=1, replica_groups=mesh['fsdp'=2,'ctx'=4,'tp'=4] {'fsdp','ctx'}, dimensions={0}, use_global_device_ids=true | all-gather | bytes 2304 | tf_op jit(solution)/shard_map/all_gather | solution.py:85
  48.1 25.5 %all_gather.45 = bf16[256,1024]{1,0:T(8,128)(2,1)S(1)} all-gather(bf16[256,128]{1,0:T(8,128)(2,1)S(1)} %copy-done.22), channel_id=1, replica_groups=mesh['fsdp'=2,'ctx'=4,'tp'=4] {'fsdp','ctx'}, dimensions={1}, use_global_device_ids=true | all-gather | bytes 589824 | tf_op jit(solution)/shard_map/all_gather | solution.py:79
  73.6 12.2 %all-gather.2 = bf16[8,1,128]{2,1,0:T(2,128)(2,1)S(1)} all-gather(bf16[1,1,128]{2,1,0:T(2,128)(2,1)S(1)} %bitcast.153), channel_id=1, replica_groups=mesh['fsdp'=2,'ctx'=4,'tp'=4] {'fsdp','ctx'}, dimensions={0}, use_global_device_ids=true | all-gather | bytes 2304 | tf_op jit(solution)/shard_map/all_gather | solution.py:86
  85.8 13.8 %all-gather.3 = bf16[8,1,128]{2,1,0:T(2,128)(2,1)S(1)} all-gather(bf16[1,1,128]{2,1,0:T(2,128)(2,1)S(1)} %bitcast.154), channel_id=1, replica_groups=mesh['fsdp'=2,'ctx'=4,'tp'=4] {'fsdp','ctx'}, dimensions={0}, use_global_device_ids=true | all-gather | bytes 2304 | tf_op jit(solution)/shard_map/all_gather | solution.py:87
  111.9 12.9 %all_gather.44 = bf16[1024,256]{0,1:T(8,128)(2,1)S(1)} all-gather(bf16[256,256]{0,1:T(8,128)(2,1)S(1)} %bitcast.131), channel_id=1, replica_groups=mesh['fsdp'=2,'ctx'=4,'tp'=4] {'ctx'}, dimensions={0}, use_global_device_ids=true | all-gather | bytes 655360 | tf_op jit(solution)/shard_map/all_gather | solution.py:135
  124.8 12.9 %fusion = (f32[4,1024]{1,0:T(4,128)S(1)}, f32[4,1024,1792]{2,1,0:T(8,128)}) fusion(pred[1024,1792]{1,0:T(8,128)(4,1)S(1)} %fusion.2, bf16[1024,4,48]{0,2,1:T(8,128)(2,1)S(1)} %slice.216, bf16[1024,4,16]{0,2,1:T(8,128)(2,1)S(1)} %get-tuple-element.57, bf16[1024,4,64]{0,2,1:T(8,128)(2,1)S(1)} %bitcast.123, bf16[1024,4,48]{0,2,1:T(8,128)(2,1)S(1)} %slice.217, ...), kind=kOutput, calls=%fused_computation.5 | convolution fusion | flops 966717440 | bytes 32784384 | tf_op jit(solution)/shard_map/qhd,khd->hqk/dot_general | solution.py:48
  137.6 13.8 %exponential_reduce_fusion = f32[4,1024]{1,0:T(4,128)S(1)} fusion(f32[4,1024,1792]{2,1,0:T(8,128)} %get-tuple-element.66, f32[4,1024]{1,0:T(4,128)S(1)} %get-tuple-element.65, pred[1024,1792]{1,0:T(8,128)(4,1)S(1)} %fusion.2), kind=kLoop, calls=%fused_computation.3 | loop fusion | flops 29356032 | bytes 31227904 | tf_op jit(solution)/shard_map/reduce_sum | solution.py:148
  151.4 12.7 %all_gather.43 = bf16[1024,256]{0,1:T(8,128)(2,1)S(1)} all-gather(bf16[256,256]{0,1:T(8,128)(2,1)S(1)} %bitcast.132), channel_id=1, replica_groups=mesh['fsdp'=2,'ctx'=4,'tp'=4] {'ctx'}, dimensions={0}, use_global_device_ids=true | all-gather | bytes 655360 | tf_op jit(solution)/shard_map/all_gather | solution.py:136
  164.2 22.0 %multiply_reduce_fusion = (f32[4,1024]{1,0:T(4,128)S(1)}, f32[4,1024,1792]{2,1,0:T(8,128)}) fusion(f32[4,1024,1792]{2,1,0:T(8,128)} %get-tuple-element.66, f32[4,1024]{1,0:T(4,128)S(1)} %log_add_fusion, pred[1024,1792]{1,0:T(8,128)(4,1)S(1)} %fusion.2, bf16[1024,4,64]{0,2,1:T(8,128)(2,1)S(1)} %bitcast.129, bf16[768,4,64]{0,2,1:T(8,128)(2,1)S(1)} %slice_bitcast_fusion.4, ...), kind=kOutput, calls=%fused_computation.1 | convolution fusion | flops 978055168 | bytes 62029824 | tf_op jit(solution)/shard_map/qhd,khd->hqk/dot_general | solution.py:186
  186.2 24.6 %multiply_convert_fusion = bf16[4,1024,1792]{2,1,0:T(8,128)(2,1)} fusion(f32[4,1024,1792]{2,1,0:T(8,128)} %get-tuple-element.69, f32[4,1024,1792]{2,1,0:T(8,128)} %get-tuple-element.66, f32[4,1024]{1,0:T(4,128)S(1)} %get-tuple-element.68, f32[4,1024]{1,0:T(4,128)S(1)} %log_add_fusion, pred[1024,1792]{1,0:T(8,128)(4,1)S(1)} %fusion.2), kind=kLoop, calls=%fused_computation | loop fusion | flops 44040192 | bytes 75268096 | tf_op jit(solution)/shard_map/convert_element_type | solution.py:190
  210.8 7.8 fusion.30
  220.7 12.7 %convolution_bitcast_fusion = f32[1792,4,64]{0,2,1:T(8,128)S(1)} fusion(bf16[1024,4,64]{0,2,1:T(8,128)(2,1)S(1)} %bitcast.130, f32[4,1024,1792]{2,1,0:T(8,128)} %get-tuple-element.66, f32[4,1024]{1,0:T(4,128)S(1)} %log_add_fusion, pred[1024,1792]{1,0:T(8,128)(4,1)S(1)} %fusion.2), kind=kOutput, calls=%fused_computation.58 | convolution fusion | flops 968884224 | bytes 33570816 | tf_op jit(solution)/shard_map/hqk,qhd->khd/dot_general | solution.py:198
  235.3 9.7 fusion.35
  246.9 14.3 %convolution_convert_fusion.1 = bf16[4,64,1024]{2,1,0:T(8,128)(2,1)} fusion(bf16[768,4,64]{0,2,1:T(8,128)(2,1)} %copy-done.13, bf16[1024,4,64]{0,2,1:T(8,128)(2,1)} %bitcast.117, f32[4,1024,1792]{2,1,0:T(8,128)} %get-tuple-element.66, f32[4,1024]{1,0:T(4,128)S(1)} %log_add_fusion, pred[1024,1792]{1,0:T(8,128)(4,1)S(1)} %fusion.2), kind=kOutput, calls=%fused_computation.75 | convolution fusion | flops 970981376 | bytes 32653312 | tf_op jit(solution)/shard_map/hqk,khd->qhd/dot_general | solution.py:150
  265.5 16.0 %multiply_convert_fusion.1 = (bf16[1024,1024]{1,0:T(8,128)(2,1)}, f32[1024,1024]{1,0:T(8,128)}, f32[1024,1024]{1,0:T(8,128)}) fusion(f32[1024]{0:T(1024)S(1)} %copy-done.26, bf16[1024,1024]{1,0:T(8,128)(2,1)} %all-gather.12.cloned.1.call-done, f32[1024]{0:T(1024)S(1)} %bitcast.148, f32[1024]{0:T(1024)S(1)} %bitcast.139, f32[1024]{0:T(1024)S(1)} %fusion.55, ...), kind=kOutput, calls=%fused_computation.41 | convolution fusion | flops 2226126848 | bytes 14700544 | tf_op jit(solution)/shard_map/dot_general | solution.py:153
  281.5 9.1 convert_reduce_fusion.2
  300.2 5.3 reduce-scatter.9.cloned.1.call-done
  313.4 6.0 convolution_convert_fusion
  322.8 5.3 fusion.31
  328.2 6.2 fusion.64
  334.5 6.4 fusion.72
  341.5 13.7 %all-gather.4 = bf16[8,1,128]{2,1,0:T(2,128)(2,1)S(1)} all-gather(bf16[1,1,128]{2,1,0:T(2,128)(2,1)S(1)} %bitcast.155), channel_id=1, replica_groups=mesh['fsdp'=2,'ctx'=4,'tp'=4] {'fsdp','ctx'}, dimensions={0}, use_global_device_ids=true | all-gather | bytes 2304 | tf_op jit(solution)/shard_map/all_gather | solution.py:82
  355.2 13.4 %all-gather.5 = bf16[8,1,128]{2,1,0:T(2,128)(2,1)S(1)} all-gather(bf16[1,1,128]{2,1,0:T(2,128)(2,1)S(1)} %bitcast.156), channel_id=1, replica_groups=mesh['fsdp'=2,'ctx'=4,'tp'=4] {'fsdp','ctx'}, dimensions={0}, use_global_device_ids=true | all-gather | bytes 2304 | tf_op jit(solution)/shard_map/all_gather | solution.py:83
  369.8 370.8 %all-reduce.16.cloned.1.call-done = (f32[1024,1024]{1,0:T(8,128)}, f32[1024,1024]{1,0:T(8,128)}, f32[1024,1024]{1,0:T(8,128)}) async-done(((f32[1024,1024]{1,0:T(8,128)}, f32[1024,1024]{1,0:T(8,128)}, f32[1024,1024]{1,0:T(8,128)}), (f32[1024,1024]{1,0:T(8,128)}, f32[1024,1024]{1,0:T(8,128)}, f32[1024,1024]{1,0:T(8,128)})) %all-reduce.16.cloned.1.call-update) | async-done | bytes 12582928 | tf_op jit(solution)/shard_map/psum | solution.py:158
  745.4 83.7 %all-reduce.14.cloned.1.call-done = bf16[1024,1024]{1,0:T(8,128)(2,1)} async-done(((bf16[1024,1024]{1,0:T(8,128)(2,1)}), bf16[1024,1024]{1,0:T(8,128)(2,1)}) %all-reduce.14.cloned.1.call-update) | async-done | bytes 2097168 | tf_op jit(solution)/shard_map/psum | solution.py:159
  829.1 9.3 fusion.18
  838.4 5.4 convert_reduce_fusion.1
  843.8 26.6 %all-reduce.9 = (f32[3,256]{1,0:T(4,128)}, f32[1024]{0:T(1024)S(1)}, f32[1024]{0:T(1024)}, f32[1024]{0:T(1024)S(1)}, f32[1024]{0:T(1024)S(1)}, /*index=5*/f32[1024]{0:T(1024)S(1)}, f32[1024]{0:T(1024)S(1)}) all-reduce(f32[3,256]{1,0:T(4,128)S(1)} %reshape.336, ...), channel_id=1, replica_groups=mesh['fsdp'=2,'ctx'=4,'tp'=4] {'fsdp','ctx'}, use_global_device_ids=true, to_apply=%region_17.18 | all-reduce | flops 6912 | bytes 55296 | tf_op jit(solution)/shard_map/psum | solution.py:254
  882.0 36.9 %reduce-scatter.11.cloned.1.call-done = f32[128,3,256]{2,0,1:T(8,128)} async-done(((f32[1024,3,256]{2,0,1:T(8,128)}), f32[128,3,256]{2,0,1:T(8,128)}) %reduce-scatter.11.cloned.1.call-update) | async-done | bytes 393232 | tf_op jit(solution)/shard_map/reduce_scatter | solution.py:244
  919.0 55.1 %reduce-scatter.15.cloned.1.call-done = f32[128,1024]{1,0:T(8,128)} async-done(((f32[1024,1024]{1,0:T(8,128)}), f32[128,1024]{1,0:T(8,128)}) %reduce-scatter.15.cloned.1.call-update) | async-done | bytes 524304 | tf_op jit(solution)/shard_map/reduce_scatter | solution.py:246
  974.1 55.6 %reduce-scatter.17.cloned.1.call-done = f32[1024,128]{1,0:T(8,128)} async-done(((f32[1024,1024]{1,0:T(8,128)}), f32[1024,128]{1,0:T(8,128)}) %reduce-scatter.17.cloned.1.call-update) | async-done | bytes 524304 | tf_op jit(solution)/shard_map/reduce_scatter | solution.py:247
  (192 shorter events, 74.1 us)
Async XLA Ops:
  7.2 10.8 %copy-start.32 = (bf16[128]{0:T(256)(128)(2,1)S(1)}, bf16[128]{0:T(256)(128)(2,1)}, u32[]{:S(2)}) copy-start(bf16[128]{0:T(256)(128)(2,1)} %param.28) | copy-start | bytes 772
  7.2 25.5 %copy-start.33 = (bf16[128]{0:T(256)(128)(2,1)S(1)}, bf16[128]{0:T(256)(128)(2,1)}, u32[]{:S(2)}) copy-start(bf16[128]{0:T(256)(128)(2,1)} %param.29) | copy-start | bytes 772
  7.2 39.3 %copy-start.30 = (bf16[3,256]{1,0:T(4,128)(2,1)S(1)}, bf16[3,256]{1,0:T(4,128)(2,1)}, u32[]{:S(2)}) copy-start(bf16[3,256]{1,0:T(4,128)(2,1)} %param.21) | copy-start | bytes 4612
  7.2 39.9 %copy-start.34 = (s32[1,3]{1,0:T(1,128)S(1)}, s32[1,3]{1,0:T(1,128)}, u32[]{:S(2)}) copy-start(s32[1,3]{1,0:T(1,128)} %param.19) | copy-start | bytes 40
  7.2 40.9 %copy-start.22 = (bf16[256,128]{1,0:T(8,128)(2,1)S(1)}, bf16[256,128]{1,0:T(8,128)(2,1)}, u32[]{:S(2)}) copy-start(bf16[256,128]{1,0:T(8,128)(2,1)} %param.22) | copy-start | bytes 196612
  7.2 66.3 %copy-start.35 = (bf16[128]{0:T(256)(128)(2,1)S(1)}, bf16[128]{0:T(256)(128)(2,1)}, u32[]{:S(2)}) copy-start(bf16[128]{0:T(256)(128)(2,1)} %param.30) | copy-start | bytes 772
  7.3 78.6 %copy-start.36 = (bf16[128]{0:T(256)(128)(2,1)S(1)}, bf16[128]{0:T(256)(128)(2,1)}, u32[]{:S(2)}) copy-start(bf16[128]{0:T(256)(128)(2,1)} %param.31) | copy-start | bytes 772
  7.3 93.0 %copy-start.31 = (bf16[1024]{0:T(1024)(128)(2,1)S(1)}, bf16[1024]{0:T(1024)(128)(2,1)}, u32[]{:S(2)}) copy-start(bf16[1024]{0:T(1024)(128)(2,1)} %param.25) | copy-start | bytes 6148
  7.3 93.6 %copy-start.6 = (bf16[1,3,256,1024]{3,2,1,0:T(8,128)(2,1)S(1)}, bf16[1,3,256,1024]{3,2,1,0:T(8,128)(2,1)}, u32[]{:S(2)}) copy-start(bf16[1,3,256,1024]{3,2,1,0:T(8,128)(2,1)} %param.33) | copy-start | bytes 4718596
  7.3 100.1 %all-gather.10.cloned.1.call-start = ((), (), s32[]{:S(2)}) async-start(), calls=%async_computation.6 | async-start | bytes 1769472 | tf_op jit(solution)/shard_map/all_gather | solution.py:78
  9.2 256.2 %all-gather.12.cloned.1.call-start = ((), (), s32[]{:S(2)}) async-start(), calls=%async_computation.7 | async-start | bytes 2359296 | tf_op jit(solution)/shard_map/all_gather | solution.py:80
  10.0 271.5 %all-gather.14.cloned.1.call-start = ((), (), s32[]{:S(2)}) async-start(), calls=%async_computation.8 | async-start | bytes 2359296 | tf_op jit(solution)/shard_map/all_gather | solution.py:81
  10.7 285.6 %reduce-scatter.7.cloned.1.call-start = ((), (), s32[]{:S(2)}) async-start(), calls=%async_computation.10 | async-start | bytes 1310720 | tf_op jit(solution)/shard_map/reduce_scatter | solution.py:202
  32.7 74.7 %copy-start.20 = (f32[8,1,128]{2,1,0:T(1,128)}, f32[8,1,128]{2,1,0:T(1,128)S(1)}, u32[]{:S(2)}) copy-start(f32[8,1,128]{2,1,0:T(1,128)S(1)} %convert_element_type.144) | copy-start | bytes 12292
  48.1 63.7 %copy-start.16 = (f32[1024,16]{0,1:T(8,128)}, f32[1024,16]{0,1:T(8,128)S(1)}, u32[]{:S(2)}) copy-start(f32[1024,16]{0,1:T(8,128)S(1)} %pad_maximum_fusion.9) | copy-start | bytes 196612
  73.6 29.9 %copy-start.11 = (bf16[256,1024]{1,0:T(8,128)(2,1)}, bf16[256,1024]{1,0:T(8,128)(2,1)S(1)}, u32[]{:S(2)}) copy-start(bf16[256,1024]{1,0:T(8,128)(2,1)S(1)} %all_gather.45) | copy-start | bytes 1572868
  111.7 52.4 %copy-start.13 = (bf16[768,4,64]{0,2,1:T(8,128)(2,1)}, bf16[768,4,64]{0,2,1:T(8,128)(2,1)S(1)}, u32[]{:S(2)}) copy-start(bf16[768,4,64]{0,2,1:T(8,128)(2,1)S(1)} %slice_bitcast_fusion.4) | copy-start | bytes 1179652
  137.6 26.6 %copy-start.18 = (bf16[1024,256]{0,1:T(8,128)(2,1)S(1)}, bf16[1024,256]{0,1:T(8,128)(2,1)}, u32[]{:S(2)}) copy-start(bf16[1024,256]{0,1:T(8,128)(2,1)} %convolution_convert_fusion.2) | copy-start | bytes 1572868
  164.2 22.0 %copy-start.9 = (bf16[1024,256]{0,1:T(8,128)(2,1)}, bf16[1024,256]{0,1:T(8,128)(2,1)S(1)}, u32[]{:S(2)}) copy-start(bf16[1024,256]{0,1:T(8,128)(2,1)S(1)} %all_gather.43) | copy-start | bytes 1572868
  246.8 58.7 %reduce-scatter.9.cloned.1.call-start = ((), (), s32[]{:S(2)}) async-start(), calls=%async_computation.11 | async-start | bytes 1310720 | tf_op jit(solution)/shard_map/reduce_scatter | solution.py:208
  265.2 475.5 %all-reduce.16.cloned.1.call-start = ((), (), s32[]{:S(2)}) async-start(), calls=%async_computation.16 | async-start | bytes 25165824 | tf_op jit(solution)/shard_map/psum | solution.py:158
  265.5 16.0 %copy-start.10 = (bf16[1,256,1024]{2,1,0:T(8,128)(2,1)S(1)}, bf16[1,256,1024]{2,1,0:T(8,128)(2,1)}, u32[]{:S(2)}) copy-start(bf16[1,256,1024]{2,1,0:T(8,128)(2,1)} %param.32) | copy-start | bytes 1572868
  281.5 10.4 %copy-start.39 = (bf16[1024,1024]{1,0:T(8,128)(2,1)S(1)}, bf16[1024,1024]{1,0:T(8,128)(2,1)}, u32[]{:S(2)}) copy-start(bf16[1024,1024]{1,0:T(8,128)(2,1)} %all-gather.12.cloned.1.call-done) | copy-start | bytes 6291460
  313.1 516.0 %all-reduce.14.cloned.1.call-start = ((), (), s32[]{:S(2)}) async-start(), calls=%async_computation.9 | async-start | bytes 4194304 | tf_op jit(solution)/shard_map/psum | solution.py:159
  319.4 562.6 %reduce-scatter.13.cloned.1.call-start = ((), (), s32[]{:S(2)}) async-start(), calls=%async_computation.13 | async-start | bytes 1179648 | tf_op jit(solution)/shard_map/reduce_scatter | solution.py:245
  322.7 596.2 %reduce-scatter.11.cloned.1.call-start = ((), (), s32[]{:S(2)}) async-start(), calls=%async_computation.12 | async-start | bytes 3538944 | tf_op jit(solution)/shard_map/reduce_scatter | solution.py:244
  328.1 646.0 %reduce-scatter.15.cloned.1.call-start = ((), (), s32[]{:S(2)}) async-start(), calls=%async_computation.14 | async-start | bytes 4718592 | tf_op jit(solution)/shard_map/reduce_scatter | solution.py:246
  334.4 695.3 %reduce-scatter.17.cloned.1.call-start = ((), (), s32[]{:S(2)}) async-start(), calls=%async_computation.15 | async-start | bytes 4718592 | tf_op jit(solution)/shard_map/reduce_scatter | solution.py:247
  340.8 14.3 %copy-start.38 = (bf16[128]{0:T(256)(128)(2,1)S(1)}, bf16[128]{0:T(256)(128)(2,1)}, u32[]{:S(2)}) copy-start(bf16[128]{0:T(256)(128)(2,1)} %param.27) | copy-start | bytes 772
  340.8 27.7 %copy-start.41 = (u32[32]{0:T(128)S(1)}, u32[32]{0:T(128)}, u32[]{:S(2)}) copy-start(u32[32]{0:T(128)} %constant.122) | copy-start | bytes 388
  829.1 9.3 copy-start.7
  870.5 159.3 %copy-start.42 = (f32[128]{0:T(128)}, f32[128]{0:T(128)S(1)}, u32[]{:S(2)}) copy-start(f32[128]{0:T(128)S(1)} %dynamic-slice.1) | copy-start | bytes 1540
  (23 other events, 101.9 us)
Sparse Core Ops, SparseCore 0:
  10.6 28.5 all-gather.9
  41.1 33.7 all-gather.11
  76.8 28.1 all-gather.13
  246.9 27.1 reduce-scatter.6
  277.7 27.7 reduce-scatter.8
  313.2 427.4 all-reduce.15
  743.6 85.4 all-reduce.13
  833.1 35.1 reduce-scatter.12
  872.7 46.2 reduce-scatter.10
  922.7 51.3 reduce-scatter.14
  978.4 51.2 reduce-scatter.16
where the time goes:
time: 1050 us; the launch traced here: 1040 us
  waiting for transfers between devices  609 us (58%)
  blocking collectives  159 us (15%)
  matrix products  150 us (14%)
  other arithmetic  76 us (7%)
  local copies, waits for them, and re-layouts  27.1 us (3%)
  between operations  15.5 us (1%)
    psum x1, waiting for transfers between devices, on_device(): attn_total = lax.psum(attn_part, 'tp')  371 us
    psum x1, waiting for transfers between devices, on_device(): lax.psum(mlp_part.astype(jnp.bfloat16), 'tp').astype(jnp.float32)  83.7 us
    reduce_scatter x1, waiting for transfers between devices, on_device(): lax.psum_scatter(grad_down, ('fsdp', 'ctx'), scatter_dimension=1, tiled=T...  55.6 us
    reduce_scatter x1, waiting for transfers between devices, on_device(): lax.psum_scatter(grad_up, ('fsdp', 'ctx'), scatter_dimension=0, tiled=True)  55.1 us
    reduce_scatter x1, waiting for transfers between devices, on_device(): lax.psum_scatter(grad_qkv, ('fsdp', 'ctx'), scatter_dimension=0, tiled=True)  36.9 us
    psum x1, blocking collectives, on_device(): lax.psum((grad_qkv_bias, grad_up_bias), ('fsdp', 'ctx'))  26.6 us
    all_gather x1, blocking collectives, on_device(): lax.all_gather(w_dense, ('fsdp', 'ctx'), axis=1, tiled=True)  25.5 us
    convert_element_type x1, other arithmetic, on_device(): grad_scores = (probs * (grad_probs - inner)).astype(jnp.bfloat16)  24.6 us
  transfers between devices with their start and end apart: 11, of which 6 were waited for; matrix products, arithmetic and copies ran while one was open for 23% of the time, Pallas kernels for 0%

commit v1 on v0

--- a/solution.py
+++ b/solution.py
@@ -74,6 +74,16 @@
     dy_prompt,
     dy_cont,
 ):
+
+    def _treat_pieces_all(named_axis, q_in):
+        how_many = jax.lax.psum(1, named_axis)
+        z = lambda current_block: [(j0, j0 ^ current_block) for j0 in range(how_many)]
+        tmp = q_in
+        for to_i in range(how_many.bit_length() - 1):
+            local_next = jax.lax.ppermute(tmp, named_axis, z(1 << to_i))
+            tmp = tmp + local_next
+        return tmp
+
     gathered = (
         lax.all_gather(w_qkv, ("fsdp", "ctx"), axis=0, tiled=True),
         lax.all_gather(w_dense, ("fsdp", "ctx"), axis=1, tiled=True),
@@ -155,7 +165,7 @@
     )
     active_low = exact_gelu(hidden).astype(jnp.bfloat16)
     mlp_part = jnp.dot(active_low, down_full, preferred_element_type=jnp.float32)
-    attn_total = lax.psum(attn_part, "tp")
+    attn_total = _treat_pieces_all("tp", q_in=attn_part)
     mlp_total = lax.psum(mlp_part.astype(jnp.bfloat16), "tp").astype(jnp.float32)
     mixed = attn_total + mlp_total
     output = inputs + mixed + dense_shift + down_shift

time: 1050 us -> 1140 us (1.086)
  waiting for transfers between devices: 609 us -> 699 us
    ppermute x0 -> x2, waiting for transfers between devices: none -> 193 us  [_treat_pieces_all(): local_next = jax.lax.ppermute(tmp, named_axis, z(1 << to_i))]
    psum x1, waiting for transfers between devices: 371 us -> 264 us  [on_device(): full_two = lax.psum(grad_norm_two, 'tp')]
    psum x1, waiting for transfers between devices: 83.7 us -> 95.1 us  [on_device(): lax.psum(mlp_part.astype(jnp.bfloat16), 'tp').astype(jnp.float32)]
  transfers between devices with their start and end apart: 11 -> 13, of which waited for: 6 -> 6; matrix products, arithmetic and copies ran while one was open for 23% -> 21% of each run, Pallas kernels for 0% -> 0%
where the time goes in v1:
time: 1140 us; the launch traced here: 1130 us
  waiting for transfers between devices  699 us (61%)
  blocking collectives  158 us (14%)
  matrix products  146 us (13%)
  other arithmetic  80.6 us (7%)
  local copies, waits for them, and re-layouts  25 us (2%)
  between operations  15.4 us (1%)
    psum x1, waiting for transfers between devices, on_device(): full_two = lax.psum(grad_norm_two, 'tp')  264 us
    ppermute x2, waiting for transfers between devices, _treat_pieces_all(): local_next = jax.lax.ppermute(tmp, named_axis, z(1 << to_i))  193 us
    psum x1, waiting for transfers between devices, on_device(): lax.psum(mlp_part.astype(jnp.bfloat16), 'tp').astype(jnp.float32)  95.1 us
    reduce_scatter x1, waiting for transfers between devices, on_device(): lax.psum_scatter(grad_down, ('fsdp', 'ctx'), scatter_dimension=1, tiled=T...  55.6 us
    reduce_scatter x1, waiting for transfers between devices, on_device(): lax.psum_scatter(grad_up, ('fsdp', 'ctx'), scatter_dimension=0, tiled=True)  55.1 us
    reduce_scatter x1, waiting for transfers between devices, on_device(): lax.psum_scatter(grad_qkv, ('fsdp', 'ctx'), scatter_dimension=0, tiled=True)  35.6 us
    psum x1, blocking collectives, on_device(): lax.psum((grad_qkv_bias, grad_up_bias), ('fsdp', 'ctx'))  26.7 us
    convert_element_type x1, other arithmetic, on_device(): grad_scores = (probs * (grad_probs - inner)).astype(jnp.bfloat16)  24.7 us
  transfers between devices with their start and end apart: 13, of which 6 were waited for; matrix products, arithmetic and copies ran while one was open for 21% of the time, Pallas kernels for 0%

profile of v1, /device:TPU:0, one launch (start us, length us, event | category | flops | bytes accessed | tf_op | source)
XLA Modules:
  0.0 1127.7 jit_solution(9808546402431840037)
XLA Ops:
  14.6 14.7 %all-gather = bf16[8,1,128]{2,1,0:T(2,128)(2,1)S(1)} all-gather(bf16[1,1,128]{2,1,0:T(2,128)(2,1)S(1)} %bitcast.150), channel_id=1, replica_groups=mesh['fsdp'=2,'ctx'=4,'tp'=4] {'fsdp','ctx'}, dimensions={0}, use_global_device_ids=true | all-gather | bytes 2304 | tf_op jit(solution)/shard_map/all_gather | solution.py:94
  29.3 13.2 %all-gather.1 = bf16[8,1,128]{2,1,0:T(2,128)(2,1)S(1)} all-gather(bf16[1,1,128]{2,1,0:T(2,128)(2,1)S(1)} %bitcast.151), channel_id=1, replica_groups=mesh['fsdp'=2,'ctx'=4,'tp'=4] {'fsdp','ctx'}, dimensions={0}, use_global_device_ids=true | all-gather | bytes 2304 | tf_op jit(solution)/shard_map/all_gather | solution.py:95
  44.1 24.6 %all_gather.45 = bf16[256,1024]{1,0:T(8,128)(2,1)S(1)} all-gather(bf16[256,128]{1,0:T(8,128)(2,1)S(1)} %copy-done.29), channel_id=1, replica_groups=mesh['fsdp'=2,'ctx'=4,'tp'=4] {'fsdp','ctx'}, dimensions={1}, use_global_device_ids=true | all-gather | bytes 589824 | tf_op jit(solution)/shard_map/all_gather | solution.py:89
  68.7 12.5 %all-gather.2 = bf16[8,1,128]{2,1,0:T(2,128)(2,1)S(1)} all-gather(bf16[1,1,128]{2,1,0:T(2,128)(2,1)S(1)} %bitcast.153), channel_id=1, replica_groups=mesh['fsdp'=2,'ctx'=4,'tp'=4] {'fsdp','ctx'}, dimensions={0}, use_global_device_ids=true | all-gather | bytes 2304 | tf_op jit(solution)/shard_map/all_gather | solution.py:96
  81.9 13.9 %all-gather.3 = bf16[8,1,128]{2,1,0:T(2,128)(2,1)S(1)} all-gather(bf16[1,1,128]{2,1,0:T(2,128)(2,1)S(1)} %bitcast.154), channel_id=1, replica_groups=mesh['fsdp'=2,'ctx'=4,'tp'=4] {'fsdp','ctx'}, dimensions={0}, use_global_device_ids=true | all-gather | bytes 2304 | tf_op jit(solution)/shard_map/all_gather | solution.py:97
  107.5 13.0 %all_gather.44 = bf16[1024,256]{0,1:T(8,128)(2,1)S(1)} all-gather(bf16[256,256]{0,1:T(8,128)(2,1)S(1)} %bitcast.131), channel_id=1, replica_groups=mesh['fsdp'=2,'ctx'=4,'tp'=4] {'ctx'}, dimensions={0}, use_global_device_ids=true | all-gather | bytes 655360 | tf_op jit(solution)/shard_map/all_gather | solution.py:145
  120.5 12.9 %fusion = (f32[4,1024]{1,0:T(4,128)S(1)}, f32[4,1024,1792]{2,1,0:T(8,128)}) fusion(pred[1024,1792]{1,0:T(8,128)(4,1)S(1)} %fusion.2, bf16[1024,4,48]{0,2,1:T(8,128)(2,1)S(1)} %slice.216, bf16[1024,4,16]{0,2,1:T(8,128)(2,1)S(1)} %get-tuple-element.56, bf16[1024,4,64]{0,2,1:T(8,128)(2,1)S(1)} %bitcast.123, bf16[1024,4,48]{0,2,1:T(8,128)(2,1)S(1)} %slice.217, ...), kind=kOutput, calls=%fused_computation.5 | convolution fusion | flops 966717440 | bytes 32784384 | tf_op jit(solution)/shard_map/qhd,khd->hqk/dot_general | solution.py:48
  133.3 13.8 %exponential_reduce_fusion = f32[4,1024]{1,0:T(4,128)S(1)} fusion(f32[4,1024,1792]{2,1,0:T(8,128)} %get-tuple-element.66, f32[4,1024]{1,0:T(4,128)S(1)} %get-tuple-element.65, pred[1024,1792]{1,0:T(8,128)(4,1)S(1)} %fusion.2), kind=kLoop, calls=%fused_computation.3 | loop fusion | flops 29356032 | bytes 31227904 | tf_op jit(solution)/shard_map/reduce_sum | solution.py:158
  147.1 12.7 %all_gather.43 = bf16[1024,256]{0,1:T(8,128)(2,1)S(1)} all-gather(bf16[256,256]{0,1:T(8,128)(2,1)S(1)} %bitcast.132), channel_id=1, replica_groups=mesh['fsdp'=2,'ctx'=4,'tp'=4] {'ctx'}, dimensions={0}, use_global_device_ids=true | all-gather | bytes 655360 | tf_op jit(solution)/shard_map/all_gather | solution.py:146
  159.8 22.0 %multiply_reduce_fusion = (f32[4,1024]{1,0:T(4,128)S(1)}, f32[4,1024,1792]{2,1,0:T(8,128)}) fusion(f32[4,1024,1792]{2,1,0:T(8,128)} %get-tuple-element.66, f32[4,1024]{1,0:T(4,128)S(1)} %log_add_fusion, pred[1024,1792]{1,0:T(8,128)(4,1)S(1)} %fusion.2, bf16[1024,4,64]{0,2,1:T(8,128)(2,1)S(1)} %bitcast.130, bf16[768,4,64]{0,2,1:T(8,128)(2,1)S(1)} %slice_bitcast_fusion.4, ...), kind=kOutput, calls=%fused_computation.1 | convolution fusion | flops 978055168 | bytes 62029824 | tf_op jit(solution)/shard_map/qhd,khd->hqk/dot_general | solution.py:196
  181.8 24.7 %multiply_convert_fusion = bf16[4,1024,1792]{2,1,0:T(8,128)(2,1)} fusion(f32[4,1024,1792]{2,1,0:T(8,128)} %get-tuple-element.68, f32[4,1024,1792]{2,1,0:T(8,128)} %get-tuple-element.66, f32[4,1024]{1,0:T(4,128)S(1)} %get-tuple-element.67, f32[4,1024]{1,0:T(4,128)S(1)} %log_add_fusion, pred[1024,1792]{1,0:T(8,128)(4,1)S(1)} %fusion.2), kind=kLoop, calls=%fused_computation | loop fusion | flops 44040192 | bytes 75268096 | tf_op jit(solution)/shard_map/convert_element_type | solution.py:200
  206.5 7.8 fusion.30
  216.5 14.0 %convolution_bitcast_fusion = f32[1792,4,64]{0,2,1:T(8,128)S(1)} fusion(bf16[1024,4,64]{0,2,1:T(8,128)(2,1)} %bitcast.129, f32[4,1024,1792]{2,1,0:T(8,128)} %get-tuple-element.66, f32[4,1024]{1,0:T(4,128)S(1)} %log_add_fusion, pred[1024,1792]{1,0:T(8,128)(4,1)S(1)} %fusion.2), kind=kOutput, calls=%fused_computation.58 | convolution fusion | flops 968884224 | bytes 33570816 | tf_op jit(solution)/shard_map/hqk,qhd->khd/dot_general | solution.py:208
  232.3 9.7 fusion.35
  244.2 15.7 %multiply_convert_fusion.1 = (bf16[1024,1024]{1,0:T(8,128)(2,1)}, f32[1024,1024]{1,0:T(8,128)}, f32[1024,1024]{1,0:T(8,128)}) fusion(f32[1024]{0:T(1024)} %convert_element_type.129, bf16[1024,1024]{1,0:T(8,128)(2,1)} %all-gather.12.cloned.1.call-done, f32[1024]{0:T(1024)} %bitcast.148, f32[1024]{0:T(1024)} %bitcast.139, f32[1024]{0:T(1024)} %copy-done.35, ...), kind=kOutput, calls=%fused_computation.41 | convolution fusion | flops 2226126848 | bytes 14700544 | tf_op jit(solution)/shard_map/dot_general | solution.py:163
  259.9 9.2 convert_reduce_fusion.2
  288.1 5.9 convolution_convert_fusion
  294.0 14.2 %convolution_convert_fusion.1 = bf16[4,64,1024]{2,1,0:T(8,128)(2,1)} fusion(bf16[768,4,64]{0,2,1:T(8,128)(2,1)} %copy-done.19, bf16[1024,4,64]{0,2,1:T(8,128)(2,1)} %bitcast.117, f32[4,1024,1792]{2,1,0:T(8,128)} %get-tuple-element.66, f32[4,1024]{1,0:T(4,128)S(1)} %log_add_fusion, pred[1024,1792]{1,0:T(8,128)(4,1)S(1)} %fusion.2), kind=kOutput, calls=%fused_computation.75 | convolution fusion | flops 970981376 | bytes 32653312 | tf_op jit(solution)/shard_map/hqk,khd->qhd/dot_general | solution.py:160
  311.9 5.3 fusion.31
  317.3 6.2 fusion.64
  327.2 192.7 %collective-permute-done = f32[1024,1024]{1,0:T(8,128)S(1)} collective-permute-done((f32[1024,1024]{1,0:T(8,128)S(1)}, f32[1024,1024]{1,0:T(8,128)S(1)}, u32[]{:S(2)}, u32[]{:S(2)}) %collective-permute-start) | collective-permute-done | bytes 4194336 | tf_op jit(solution)/shard_map/ppermute | solution.py:83
  528.4 13.6 %all-gather.4 = bf16[8,1,128]{2,1,0:T(2,128)(2,1)S(1)} all-gather(bf16[1,1,128]{2,1,0:T(2,128)(2,1)S(1)} %bitcast.155), channel_id=1, replica_groups=mesh['fsdp'=2,'ctx'=4,'tp'=4] {'fsdp','ctx'}, dimensions={0}, use_global_device_ids=true | all-gather | bytes 2304 | tf_op jit(solution)/shard_map/all_gather | solution.py:92
  541.9 13.1 %all-gather.5 = bf16[8,1,128]{2,1,0:T(2,128)(2,1)S(1)} all-gather(bf16[1,1,128]{2,1,0:T(2,128)(2,1)S(1)} %bitcast.156), channel_id=1, replica_groups=mesh['fsdp'=2,'ctx'=4,'tp'=4] {'fsdp','ctx'}, dimensions={0}, use_global_device_ids=true | all-gather | bytes 2304 | tf_op jit(solution)/shard_map/all_gather | solution.py:93
  556.4 263.6 %all-reduce.16.cloned.1.call-done = (f32[1024,1024]{1,0:T(8,128)}, f32[1024,1024]{1,0:T(8,128)}) async-done(((f32[1024,1024]{1,0:T(8,128)}, f32[1024,1024]{1,0:T(8,128)}), (f32[1024,1024]{1,0:T(8,128)}, f32[1024,1024]{1,0:T(8,128)})) %all-reduce.16.cloned.1.call-update) | async-done | bytes 8388624 | tf_op jit(solution)/shard_map/psum | solution.py:248
  820.0 4.7 fusion.76
  824.7 95.1 %all-reduce.14.cloned.1.call-done = bf16[1024,1024]{1,0:T(8,128)(2,1)} async-done(((bf16[1024,1024]{1,0:T(8,128)(2,1)}), bf16[1024,1024]{1,0:T(8,128)(2,1)}) %all-reduce.14.cloned.1.call-update) | async-done | bytes 2097168 | tf_op jit(solution)/shard_map/psum | solution.py:169
  919.8 10.4 fusion.18
  930.2 5.4 convert_reduce_fusion.1
  935.6 26.7 %all-reduce.9 = (f32[3,256]{1,0:T(4,128)}, f32[1024]{0:T(1024)S(1)}, f32[1024]{0:T(1024)}, f32[1024]{0:T(1024)S(1)}, f32[1024]{0:T(1024)S(1)}, /*index=5*/f32[1024]{0:T(1024)S(1)}, f32[1024]{0:T(1024)S(1)}) all-reduce(f32[3,256]{1,0:T(4,128)S(1)} %reshape.336, ...), channel_id=1, replica_groups=mesh['fsdp'=2,'ctx'=4,'tp'=4] {'fsdp','ctx'}, use_global_device_ids=true, to_apply=%region_16.17 | all-reduce | flops 6912 | bytes 55296 | tf_op jit(solution)/shard_map/psum | solution.py:264
  974.1 35.6 %reduce-scatter.11.cloned.1.call-done = f32[128,3,256]{2,0,1:T(8,128)} async-done(((f32[1024,3,256]{2,0,1:T(8,128)}), f32[128,3,256]{2,0,1:T(8,128)}) %reduce-scatter.11.cloned.1.call-update) | async-done | bytes 393232 | tf_op jit(solution)/shard_map/reduce_scatter | solution.py:254
  1009.7 55.1 %reduce-scatter.15.cloned.1.call-done = f32[128,1024]{1,0:T(8,128)} async-done(((f32[1024,1024]{1,0:T(8,128)}), f32[128,1024]{1,0:T(8,128)}) %reduce-scatter.15.cloned.1.call-update) | async-done | bytes 524304 | tf_op jit(solution)/shard_map/reduce_scatter | solution.py:256
  1064.8 55.6 %reduce-scatter.17.cloned.1.call-done = f32[1024,128]{1,0:T(8,128)} async-done(((f32[1024,1024]{1,0:T(8,128)}), f32[1024,128]{1,0:T(8,128)}) %reduce-scatter.17.cloned.1.call-update) | async-done | bytes 524304 | tf_op jit(solution)/shard_map/reduce_scatter | solution.py:257
  (221 shorter events, 74.8 us)
Async XLA Ops:
  7.2 35.3 %copy-start.42 = (bf16[3,256]{1,0:T(4,128)(2,1)S(1)}, bf16[3,256]{1,0:T(4,128)(2,1)}, u32[]{:S(2)}) copy-start(bf16[3,256]{1,0:T(4,128)(2,1)} %param.21) | copy-start | bytes 4612
  7.2 35.3 %copy-start.46 = (s32[1,3]{1,0:T(1,128)S(1)}, s32[1,3]{1,0:T(1,128)}, u32[]{:S(2)}) copy-start(s32[1,3]{1,0:T(1,128)} %param.19) | copy-start | bytes 40
  7.2 36.9 %copy-start.29 = (bf16[256,128]{1,0:T(8,128)(2,1)S(1)}, bf16[256,128]{1,0:T(8,128)(2,1)}, u32[]{:S(2)}) copy-start(bf16[256,128]{1,0:T(8,128)(2,1)} %param.22) | copy-start | bytes 196612
  7.2 61.5 %copy-start.47 = (bf16[128]{0:T(256)(128)(2,1)S(1)}, bf16[128]{0:T(256)(128)(2,1)}, u32[]{:S(2)}) copy-start(bf16[128]{0:T(256)(128)(2,1)} %param.30) | copy-start | bytes 772
  7.3 74.6 %copy-start.48 = (bf16[128]{0:T(256)(128)(2,1)S(1)}, bf16[128]{0:T(256)(128)(2,1)}, u32[]{:S(2)}) copy-start(bf16[128]{0:T(256)(128)(2,1)} %param.31) | copy-start | bytes 772
  7.3 89.1 %copy-start.43 = (bf16[1024]{0:T(1024)(128)(2,1)S(1)}, bf16[1024]{0:T(1024)(128)(2,1)}, u32[]{:S(2)}) copy-start(bf16[1024]{0:T(1024)(128)(2,1)} %param.25) | copy-start | bytes 6148
  7.3 89.7 %copy-start.5 = (bf16[1,3,256,1024]{3,2,1,0:T(8,128)(2,1)S(1)}, bf16[1,3,256,1024]{3,2,1,0:T(8,128)(2,1)}, u32[]{:S(2)}) copy-start(bf16[1,3,256,1024]{3,2,1,0:T(8,128)(2,1)} %param.33) | copy-start | bytes 4718596
  7.3 95.3 %all-gather.10.cloned.1.call-start = ((), (), s32[]{:S(2)}) async-start(), calls=%async_computation.6 | async-start | bytes 1769472 | tf_op jit(solution)/shard_map/all_gather | solution.py:88
  9.2 234.9 %all-gather.12.cloned.1.call-start = ((), (), s32[]{:S(2)}) async-start(), calls=%async_computation.7 | async-start | bytes 2359296 | tf_op jit(solution)/shard_map/all_gather | solution.py:90
  10.0 249.8 %all-gather.14.cloned.1.call-start = ((), (), s32[]{:S(2)}) async-start(), calls=%async_computation.8 | async-start | bytes 2359296 | tf_op jit(solution)/shard_map/all_gather | solution.py:91
  10.7 264.0 %reduce-scatter.7.cloned.1.call-start = ((), (), s32[]{:S(2)}) async-start(), calls=%async_computation.10 | async-start | bytes 1310720 | tf_op jit(solution)/shard_map/reduce_scatter | solution.py:212
  12.8 89.8 %copy-start.27 = (f32[1024]{0:T(1024)}, f32[1024]{0:T(1024)S(1)}, u32[]{:S(2)}) copy-start(f32[1024]{0:T(1024)S(1)} %broadcast_multiply_fusion) | copy-start | bytes 12292
  14.5 82.4 %copy-start.33 = (f32[1024]{0:T(1024)}, f32[1024]{0:T(1024)S(1)}, u32[]{:S(2)}) copy-start(f32[1024]{0:T(1024)S(1)} %fusion.19) | copy-start | bytes 12292
  14.6 88.0 %copy-start.35 = (f32[1024]{0:T(1024)}, f32[1024]{0:T(1024)S(1)}, u32[]{:S(2)}) copy-start(f32[1024]{0:T(1024)S(1)} %fusion.55) | copy-start | bytes 12292
  29.3 73.3 %copy-start.30 = (f32[8,1,128]{2,1,0:T(1,128)}, f32[8,1,128]{2,1,0:T(1,128)S(1)}, u32[]{:S(2)}) copy-start(f32[8,1,128]{2,1,0:T(1,128)S(1)} %convert_element_type.144) | copy-start | bytes 12292
  42.5 60.1 %copy-start.39 = (f32[8,1,128]{2,1,0:T(1,128)}, f32[8,1,128]{2,1,0:T(1,128)S(1)}, u32[]{:S(2)}) copy-start(f32[8,1,128]{2,1,0:T(1,128)S(1)} %convert_element_type.145) | copy-start | bytes 12292
  68.7 30.8 %copy-start.15 = (bf16[256,1024]{1,0:T(8,128)(2,1)}, bf16[256,1024]{1,0:T(8,128)(2,1)S(1)}, u32[]{:S(2)}) copy-start(bf16[256,1024]{1,0:T(8,128)(2,1)S(1)} %all_gather.45) | copy-start | bytes 1572868
  107.0 52.9 %copy-start.19 = (bf16[768,4,64]{0,2,1:T(8,128)(2,1)}, bf16[768,4,64]{0,2,1:T(8,128)(2,1)S(1)}, u32[]{:S(2)}) copy-start(bf16[768,4,64]{0,2,1:T(8,128)(2,1)S(1)} %slice_bitcast_fusion.4) | copy-start | bytes 1179652
  216.4 63.5 %reduce-scatter.9.cloned.1.call-start = ((), (), s32[]{:S(2)}) async-start(), calls=%async_computation.11 | async-start | bytes 1310720 | tf_op jit(solution)/shard_map/reduce_scatter | solution.py:218
  243.9 576.1 %all-reduce.16.cloned.1.call-start = ((), (), s32[]{:S(2)}) async-start(), calls=%async_computation.16 | async-start | bytes 16777216 | tf_op jit(solution)/shard_map/psum | solution.py:248
  287.6 632.2 %all-reduce.14.cloned.1.call-start = ((), (), s32[]{:S(2)}) async-start(), calls=%async_computation.9 | async-start | bytes 4194304 | tf_op jit(solution)/shard_map/psum | solution.py:169
  294.0 680.1 %reduce-scatter.13.cloned.1.call-start = ((), (), s32[]{:S(2)}) async-start(), calls=%async_computation.13 | async-start | bytes 1179648 | tf_op jit(solution)/shard_map/reduce_scatter | solution.py:255
  311.8 697.9 %reduce-scatter.11.cloned.1.call-start = ((), (), s32[]{:S(2)}) async-start(), calls=%async_computation.12 | async-start | bytes 3538944 | tf_op jit(solution)/shard_map/reduce_scatter | solution.py:254
  317.2 747.6 %reduce-scatter.15.cloned.1.call-start = ((), (), s32[]{:S(2)}) async-start(), calls=%async_computation.14 | async-start | bytes 4718592 | tf_op jit(solution)/shard_map/reduce_scatter | solution.py:256
  323.5 797.0 %reduce-scatter.17.cloned.1.call-start = ((), (), s32[]{:S(2)}) async-start(), calls=%async_computation.15 | async-start | bytes 4718592 | tf_op jit(solution)/shard_map/reduce_scatter | solution.py:257
  325.4 197.9 %copy-start.6 = (bf16[1,3,256,1024]{3,2,1,0:T(8,128)(2,1)S(1)}, bf16[1,3,256,1024]{3,2,1,0:T(8,128)(2,1)}, u32[]{:S(2)}) copy-start(bf16[1,3,256,1024]{3,2,1,0:T(8,128)(2,1)} %param.33) | copy-start | bytes 4718596
  325.4 197.8 %copy-start.12 = (bf16[1,256,1024]{2,1,0:T(8,128)(2,1)S(1)}, bf16[1,256,1024]{2,1,0:T(8,128)(2,1)}, u32[]{:S(2)}) copy-start(bf16[1,256,1024]{2,1,0:T(8,128)(2,1)} %param.32) | copy-start | bytes 1572868
  325.4 197.8 %copy-start.17 = (bf16[1024,1024]{1,0:T(8,128)(2,1)S(1)}, bf16[1024,1024]{1,0:T(8,128)(2,1)}, u32[]{:S(2)}) copy-start(bf16[1024,1024]{1,0:T(8,128)(2,1)} %get-tuple-element.37) | copy-start | bytes 6291460
  325.4 194.5 %collective-permute-start = (f32[1024,1024]{1,0:T(8,128)S(1)}, f32[1024,1024]{1,0:T(8,128)S(1)}, u32[]{:S(2)}, u32[]{:S(2)}) collective-permute-start(f32[1024,1024]{1,0:T(8,128)S(1)} %fusion.78), channel_id=1, source_target_pairs={{0,1},{1,0},{2,3},{3,2},{4,5},{5,4},{6,7},{7,6},{8,9},{9,8},{10,11... | collective-permute-start | bytes 12582920 | tf_op jit(solution)/shard_map/ppermute | solution.py:83
  522.8 397.0 %collective-permute-start.1 = (f32[1024,1024]{1,0:T(8,128)}, f32[1024,1024]{1,0:T(8,128)}, u32[]{:S(2)}, u32[]{:S(2)}) collective-permute-start(f32[1024,1024]{1,0:T(8,128)} %add.177), channel_id=1, source_target_pairs={{0,2},{1,3},{2,0},{3,1},{4,6},{5,7},{6,4},{7,5},{8,10},{9,11},{10,... | collective-permute-start | bytes 12582920 | tf_op jit(solution)/shard_map/ppermute | solution.py:83
  527.7 27.4 %copy-start.53 = (u32[32]{0:T(128)S(1)}, u32[32]{0:T(128)}, u32[]{:S(2)}) copy-start(u32[32]{0:T(128)} %constant.122) | copy-start | bytes 388
  962.4 158.0 %copy-start.54 = (f32[128]{0:T(128)}, f32[128]{0:T(128)S(1)}, u32[]{:S(2)}) copy-start(f32[128]{0:T(128)S(1)} %dynamic-slice.1) | copy-start | bytes 1540
  (37 other events, 286.2 us)
Sparse Core Ops, SparseCore 0:
  10.6 28.5 all-gather.9
  41.1 32.1 all-gather.11
  75.2 28.1 all-gather.13
  216.5 27.5 reduce-scatter.6
  247.7 27.7 reduce-scatter.8
  287.8 532.1 all-reduce.15
  822.9 96.8 all-reduce.13
  923.9 35.2 reduce-scatter.12
  963.5 46.1 reduce-scatter.10
  1013.5 51.3 reduce-scatter.14
  1069.1 51.2 reduce-scatter.16
